TPU v7x, 32 devices: a whole 2x2x4 slice. The times are simulated.
32 devices in a mesh: scan: 2 (over y), angle: 16 (over z, x, core).
Axes of the slice: x: 2, y: 2, z: 4, core: 2. Of those that a mesh axis runs over, the one named last changes fastest.
Arguments:
- object_init: float32 [32, 2, 128, 1024], P(('scan', 'angle')), parts along dimension 0, may hold values from -3.6 to 3.6
- measured: bfloat16 [32, 15, 128, 128], P(('scan', 'angle')), parts along dimension 0
- positions: int32 [32, 15, 2], P(('scan', 'angle')), parts along dimension 0, may hold values from 0 to 896, as said below
- angle_list: int32 [32], P('scan'), parts along dimension 0, may hold values from 0 to 15, each once
- probe: float32 [4, 128, 128], P('scan'), parts along dimension 0, may hold values from -3 to 3
- radial: float32 [16, 1024, 1024], P('angle'), may hold values from -0.1875 to 0.1875
Outputs:
- slices: float32 [32, 2, 128, 1024], P(('scan', 'angle')), parts along dimension 0
- probe_out: float32 [4, 128, 128], P('scan'), parts along dimension 0
There are 2 independent parts, one for each index of `scan`. A program takes and returns all parts, laid end to end along the dimension named above; an argument that names none is the same for every part. Nothing has to cross between parts.
Inputs may be any that keep to these rules, and one draw needn't show every extreme that they name: `positions`: for each angle, patch number n = r * 15 + c has offsets (r * 64, c * 64) moved by at most 8 cells in each dimension and clipped so that the patch lies inside the 128 x 1024 projection.
All inputs are finite; a program needn't handle non-finite values.
Results may differ from a plain program's by a relative error of at most 0.0014.
The roundings to bfloat16 on the way count: a program that leaves them out, or rounds other values in their place, can miss the bound.
Values sent between devices are 32-bit elements; how exact they have to be, the bound alone decides.
No kernel may reach another device: no remote copies, remote signals or barrier semaphores. Data moves between devices by JAX's collectives and lax.ppermute only.
A program may use at most 64 MiB of HBM per device.

v0:
```python
import functools
import math

import jax
import jax.numpy as jnp
import numpy as np
from jax import lax
from jax.experimental import pallas as pl
from jax.experimental.pallas import tpu as pltpu
from jax.sharding import PartitionSpec as P


LANES = 128
SUBLANES = 8

object_rate = 0.5
probe_rate = 1.0

VMEM = pl.BlockSpec(memory_space=pltpu.VMEM)
SMEM = pl.BlockSpec(memory_space=pltpu.SMEM)


def transform_tables(size):
    index = np.arange(size, dtype=np.int32)
    phase = index[:, None] * index[None, :] % size
    angle = phase.astype(np.float32) * np.float32(2.0 * math.pi / size)
    scale = np.float32(1.0 / math.sqrt(size))
    c = (np.cos(angle) * scale).astype(jnp.bfloat16)
    s = (np.sin(angle) * scale).astype(jnp.bfloat16)
    t = np.block([[c, s], [-s, c]])
    return jnp.asarray(t), jnp.asarray(np.ascontiguousarray(t.T))


def dot(a, b):
    return jnp.dot(a, b, preferred_element_type=jnp.float32)


def window(pos, n, tiles):
    col = pos[1, n]
    q = jnp.minimum(col // LANES, tiles - 2)
    rem = col - q * LANES
    return q, rem


def cut(load, q, rem, mask):
    y = jnp.where(mask, load(q), load(q + 1))
    return pltpu.roll(y, lax.rem(LANES - rem, LANES), 1)


def iterate(pos, piece, measured, probe, t1, t2, out, pg):
    size = probe.shape[1]
    patches = measured.shape[0]
    tiles = out.shape[0] // (size // SUBLANES)
    view = out.reshape(size // SUBLANES, tiles, 2, SUBLANES, LANES)
    lane = lax.broadcasted_iota(jnp.int32, (size, LANES), 1)
    prb_re, prb_im = probe[0], probe[1]
    rate = object_rate / jnp.max(prb_re * prb_re + prb_im * prb_im)

    def both(a, b):
        return jnp.concatenate([a.astype(jnp.bfloat16), b.astype(jnp.bfloat16)], 0)

    def regroup(x):
        x = x.astype(jnp.bfloat16)
        spans = [slice(i * size, (i + 1) * size) for i in range(patches)]
        return jnp.concatenate([jnp.concatenate([x[:size, p], x[size:, p]], 1) for p in spans], 0)

    waves = []
    for n in range(patches):
        a, b = piece(n)
        waves.append(both(prb_re * a - prb_im * b, prb_re * b + prb_im * a))
    half = regroup(dot(t1[...], jnp.concatenate(waves, 1)))
    far = dot(half, t2[...])
    pushes = []
    for n in range(patches):
        rows = slice(n * size, (n + 1) * size)
        fr, fi = far[rows, :size], far[rows, size:]
        resid = fr * fr + fi * fi - measured[n].astype(jnp.float32)
        pushes.append(both(resid * fr, resid * fi))
    back = regroup(dot(t2[...], jnp.concatenate(pushes, 1)))
    grad = dot(back, t1[...])
    total_re = total_im = 0.0
    step_re, step_im = prb_re * rate, prb_im * rate
    for n in range(patches):
        rows = slice(n * size, (n + 1) * size)
        gr, gi = grad[rows, :size], grad[rows, size:]
        a, b = piece(n)
        total_re, total_im = total_re + (a * gr + b * gi), total_im + (a * gi - b * gr)
        q, rem = window(pos, n, tiles)
        mask = lane >= rem
        for c, value in ((0, step_re * gr + step_im * gi), (1, step_re * gi - step_im * gr)):
            r = pltpu.roll(value, lax.rem(rem, LANES), 1)
            for t, part in ((q, jnp.where(mask, r, 0.0)), (q + 1, jnp.where(mask, 0.0, r))):
                view[:, t, c] = view[:, t, c] - part.reshape(size // SUBLANES, SUBLANES, LANES)
    pg[:size] = total_re
    pg[size : 2 * size] = total_im


def energy_of(piece, patches):
    total = 0.0
    for n in range(patches):
        for x in piece(n):
            total = total + (x * x).reshape(-1, SUBLANES, LANES).sum(0)
    return total


def hand_out(low, pg, parts):
    height = parts[0].shape[0] - SUBLANES
    for m, part in enumerate(parts):
        start = pl.multiple_of((low[0] ^ m) * height, SUBLANES)
        part[:height] = pg[pl.ds(start, height)]
        part[height:] = pg[height * len(parts) :]


def collect(low, blocks, probe, out):
    height = blocks[0].shape[0] - SUBLANES
    size = probe.shape[1]
    energy = jnp.sum(blocks[0][height:]) / (size * size)
    share = min(height, size)
    for m, block in enumerate(blocks):
        for piece in range(height // share):
            start = (low[0] ^ m) * height + piece * share
            where = (start // size, pl.ds(pl.multiple_of(start % size, SUBLANES), share))
            gradient = block[piece * share : piece * share + share]
            out[where] = probe[where] - probe_rate * gradient / energy


def first_kernel(inner, low, pos, obj_far, measured_far, probe_far, t1_far, t2_far, out, *refs):
    parts, (obj, measured, probe, t1, t2, pieces, pg, sem) = refs[:inner], refs[inner:]
    pairs = ((probe_far, probe), (obj_far, obj), (t1_far, t1), (t2_far, t2), (measured_far, measured))
    copies = [pltpu.make_async_copy(far, near, sem.at[i]) for i, (far, near) in enumerate(pairs)]
    for copy in copies:
        copy.start()
    size = probe.shape[1]
    patches, tiles = measured.shape[0], obj.shape[2] // LANES
    lane = lax.broadcasted_iota(jnp.int32, (size, LANES), 1)
    copies[0].wait()
    copies[1].wait()
    for n in range(patches):
        q, rem = window(pos, n, tiles)
        mask = lane >= rem
        for c in range(2):

            def load(t):
                return obj[c, :, pl.ds(pl.multiple_of(t * LANES, LANES), LANES)]

            pieces[n, c] = cut(load, q, rem, mask)
    for r in range(size // SUBLANES):
        for t in range(tiles):
            for c in range(2):
                out[r * tiles + t, c] = obj[c, r * 8 : r * 8 + 8, t * 128 : t * 128 + 128]

    def piece(n):
        return pieces[n, 0], pieces[n, 1]

    pg[2 * size :] = energy_of(piece, patches)
    for copy in copies[2:]:
        copy.wait()
    iterate(pos, piece, measured, probe, t1, t2, out, pg)
    hand_out(low, pg, parts)


def cut_kernel(pos, obj, pieces, energy):
    patches, _, size, _ = pieces.shape
    tiles = obj.shape[0] // (size // SUBLANES)
    view = obj.reshape(size // SUBLANES, tiles, 2, SUBLANES, LANES)
    lane = lax.broadcasted_iota(jnp.int32, (size, LANES), 1)
    energy[...] = jnp.zeros_like(energy)

    def body(n, carry):
        q, rem = window(pos, n, tiles)
        mask = lane >= rem
        for c in range(2):
            x = cut(lambda t: view[:, t, c].reshape(size, LANES), q, rem, mask)
            pieces[n, c] = x
            energy[...] += (x * x).reshape(-1, SUBLANES, LANES).sum(0)
        return carry

    lax.fori_loop(0, patches, body, 0)


def second_kernel(inner, low, pos, obj, pieces, energy, measured, probe, t1, t2, *refs):
    blocks, (prb_out, out), parts, pg = refs[:inner], refs[inner : inner + 2], refs[inner + 2 : -1], refs[-1]
    size = probe.shape[1]
    collect(low, blocks, probe, prb_out)
    pg[2 * size :] = energy[...]
    out[...] = obj[...]
    iterate(pos, lambda n: (pieces[n, 0], pieces[n, 1]), measured, prb_out, t1, t2, out, pg)
    hand_out(low, pg, parts)


def probe_kernel(low, probe, *refs):
    collect(low, refs[:-1], probe, refs[-1])


def butterfly(values):
    n = len(values)
    if n == 1:
        return values
    even, odd = butterfly(values[::2]), butterfly(values[1::2])
    low, high = [], []
    for k in range(n // 2):
        (er, ei), (xr, xi) = even[k], odd[k]
        c, s = math.cos(2 * math.pi * k / n), -math.sin(2 * math.pi * k / n)
        if k == 0:
            tr, ti = xr, xi
        elif 4 * k == n:
            tr, ti = xi, -xr
        elif 8 * k == n:
            tr, ti = (xr + xi) * c, (xi - xr) * c
        elif 8 * k == 3 * n:
            tr, ti = (xr * c - xi * s), (xr * s + xi * c)
        else:
            tr, ti = xr * c - xi * s, xr * s + xi * c
        low.append((er + tr, ei + ti))
        high.append((er - tr, ei - ti))
    return low + high


def angular_kernel(angles, blocks, out, where):
    count = blocks.shape[0]

    def note(b, carry):
        where[angles[b]] = b
        return carry

    lax.fori_loop(0, count, note, 0)
    scale = 1.0 / math.sqrt(count)

    def cell(j, carry):
        values = []
        for a in range(count):
            block = blocks[where[a], j]
            values.append((block[0] * scale, block[1] * scale))
        for k, (re, im) in enumerate(butterfly(values)):
            out[k, j, 0] = re
            out[k, j, 1] = im
        return carry

    lax.fori_loop(0, blocks.shape[1], cell, 0)


def split(x):
    high = x.astype(jnp.bfloat16)
    return high, (x - high.astype(jnp.float32)).astype(jnp.bfloat16)


def prepare_kernel(radial, high, low):
    high[...], low[...] = split(radial[...])


def invert_kernel(harm, r_high, r_low_far, out, x_high, x_low, r_low, sem):
    copy = pltpu.make_async_copy(r_low_far, r_low, sem)
    copy.start()
    cells, _, rows, lanes = harm.shape
    tiles = r_high.shape[0] // lanes
    height = cells // tiles * rows
    for r in range(cells // tiles):
        for t in range(tiles):
            for c in range(2):
                where = (slice(c * height + r * 8, c * height + r * 8 + 8), slice(t * 128, t * 128 + 128))
                x_high[where], x_low[where] = split(harm[r * tiles + t, c])
    value = dot(x_high[...], r_high[...]) + dot(x_low[...], r_high[...])
    copy.wait()
    out[...] = (value + dot(x_high[...], r_low[...])).reshape(out.shape)


HBM = pltpu.MemorySpace.HBM


def call(kernel, out_shape, args, scratch=(), flops=0, scalars=0, far=(), limit=2):
    moved = sum(math.prod(x.shape) * x.dtype.itemsize for x in (*args, *jax.tree.leaves(out_shape)))
    specs = [SMEM] * scalars + [VMEM] * (len(args) - scalars)
    args = list(args)
    for i in far:
        args[i] = pltpu.with_memory_space_constraint(args[i], HBM)
        if i >= scalars:
            specs[i] = pl.BlockSpec(memory_space=HBM)
    return pl.pallas_call(
        kernel,
        out_shape=out_shape,
        in_specs=specs,
        out_specs=jax.tree.map(lambda _: VMEM, out_shape),
        scratch_shapes=scratch,
        cost_estimate=pl.CostEstimate(flops=flops, bytes_accessed=moved, transcendentals=0),
        compiler_params=pltpu.CompilerParams(vmem_limit_bytes=limit << 20),
    )(*args)


def merge_kernel(*refs):
    total = refs[0][...]
    for x in refs[1:-1]:
        total = total + x[...]
    refs[-1][...] = total


def merge(parts):
    return call(merge_kernel, jax.ShapeDtypeStruct(parts[0].shape, parts[0].dtype), parts)


def all_sum(parts, axis, count):
    inner = len(parts)
    outer = count // inner

    def swap(x, mask):
        return lax.ppermute(x, axis, [(i, i ^ mask) for i in range(count)])

    others = [swap(parts[m], m) for m in range(1, inner)]
    total = merge([parts[0], *others])
    others = [swap(total, m * inner) for m in range(1, outer)]
    total = merge([total, *others])
    return [total] + [swap(total, m) for m in range(1, inner)]


def on_device(count, object_init, measured, positions, angle_list, probe, radial):
    f32, bf16 = jnp.float32, jnp.bfloat16
    shape = jax.ShapeDtypeStruct
    size = probe.shape[1]
    rows, columns = object_init.shape[2:]
    cells = rows // SUBLANES * (columns // LANES)
    patches = measured.shape[1]
    assert object_init.shape[0] == 1 and rows == size == LANES and cells % count == 0
    t1, t2 = transform_tables(size)
    obj, meas, pos = object_init[0], measured[0], positions[0].T
    flops = patches * 4 * 2 * (2 * size) * (2 * size) * size
    inner = 1 << (count.bit_length() // 2)
    low = (lax.axis_index("angle") & (inner - 1)).reshape(1)
    messages = [shape((2 * size // inner + SUBLANES, LANES), f32)] * inner
    field = shape((cells, 2, SUBLANES, LANES), f32)
    windows = (patches, 2, size, LANES)
    gradient = pltpu.VMEM((2 * size + SUBLANES, LANES), f32)
    obj, *parts = call(
        functools.partial(first_kernel, inner),
        [field, *messages],
        (low, pos, obj, meas, probe, t1, t2),
        [pltpu.VMEM(x.shape, x.dtype) for x in (obj, meas, probe, t1, t2)]
        + [pltpu.VMEM(windows, f32), gradient, pltpu.SemaphoreType.DMA((5,))],
        flops,
        2,
        far=range(1, 7),
        limit=16,
    )
    pieces, energy = call(
        cut_kernel, [shape(windows, f32), shape((SUBLANES, LANES), f32)], (pos, obj), (), 10 * obj.size, 1
    )
    r_high, r_low = call(prepare_kernel, [shape(radial.shape[1:], bf16)] * 2, (radial[0],), flops=3 * radial.size)
    blocks = all_sum(parts, "angle", count)
    prb, obj, *parts = call(
        functools.partial(second_kernel, inner),
        [shape(probe.shape, f32), field, *messages],
        (low, pos, obj, pieces, energy, meas, probe, t1, t2, *blocks),
        [gradient],
        flops,
        2,
        limit=16,
    )

    def exchange(x):
        return lax.all_to_all(x, "angle", split_axis=0, concat_axis=0, tiled=True)

    received = exchange(obj)
    grouped = shape((count, cells // count, 2, SUBLANES, LANES), f32)
    harm = call(
        angular_kernel,
        grouped,
        (angle_list, received.reshape(grouped.shape)),
        [pltpu.SMEM((count,), jnp.int32)],
        10 * received.size,
        1,
        limit=8,
    ).reshape(field.shape)
    harm = exchange(harm)
    slices = call(
        invert_kernel,
        shape(object_init.shape[1:], f32),
        (harm, r_high, r_low),
        [pltpu.VMEM((2 * rows, columns), bf16)] * 2
        + [pltpu.VMEM(r_low.shape, bf16), pltpu.SemaphoreType.DMA],
        6 * 2 * rows * columns * columns,
        0,
        far=(2,),
        limit=12,
    )
    blocks = all_sum(parts, "angle", count)
    probe_out = call(probe_kernel, shape(probe.shape, f32), (low, prb, *blocks), scalars=1)
    return slices[None], probe_out


def solution(mesh):
    count = mesh.shape["angle"]

    def body(*args):
        return on_device(count, *args)

    in_specs = (
        P(("scan", "angle"), None, None, None),
        P(("scan", "angle"), None, None, None),
        P(("scan", "angle"), None, None),
        P("scan"),
        P("scan", None, None),
        P("angle", None, None),
    )
    out_specs = (P(("scan", "angle"), None, None, None), P("scan", None, None))
    return jax.shard_map(body, mesh=mesh, in_specs=in_specs, out_specs=out_specs, check_vma=False)
```

profile of v0, /device:TPU:0, one launch (start us, length us, event | category | flops | bytes accessed | tf_op | source)
XLA Modules:
  0.0 103.5 jit_solution(5016469499088505166)
XLA Ops:
  0.6 0.0 copy-start.6
  0.6 0.0 copy-start.2
  0.7 0.0 copy-start.3
  0.7 0.0 copy-start.4
  0.7 0.0 copy-start.5
  0.7 4.8 %shard_map.95 = (f32[128,2,8,128]{3,2,1,0:T(8,128)S(1)}, f32[72,128]{1,0:T(8,128)S(1)}, f32[72,128]{1,0:T(8,128)S(1)}, f32[72,128]{1,0:T(8,128)S(1)}, f32[72,128]{1,0:T(8,128)S(1)}) custom-call(s32[1]{0:T(128)} %bitcast.low, s32[2,15]{1,0:T(2,128)} %bitcast.14, f32[2,128,1024]{2,1,0:T(8,128)} %bitcast.18, bf16[15,128,128]{2,1,0:T(8,128)(2,1)} %bitcast.12, ...), custom_call_target="tpu_custom_call" | custom-call | flops 1006632960 | bytes 3129468 | tf_op jit(solution)/shard_map/pallas_call | solution.py:278
  5.5 0.6 collective-permute-start
  6.1 2.5 %collective-permute-start.1 = (f32[72,128]{1,0:T(8,128)S(1)}, f32[72,128]{1,0:T(8,128)S(1)}, u32[]{:S(2)}, u32[]{:S(2)}) collective-permute-start(f32[72,128]{1,0:T(8,128)S(1)} %get-tuple-element.22), channel_id=1, source_target_pairs={{0,2},{1,3},{2,0},{3,1},{4,6},{5,7},{6,4},{7,5},{8,10},{9,11},{10,... | collective-permute-start | bytes 110600 | tf_op jit(solution)/shard_map/ppermute | solution.py:305
  8.6 0.0 collective-permute-start.2
  8.7 0.0 collective-permute-done.refs_1_
  8.7 2.0 %collective-permute-done.1.refs_2_ = f32[72,128]{1,0:T(8,128)S(1)} collective-permute-done((f32[72,128]{1,0:T(8,128)S(1)}, f32[72,128]{1,0:T(8,128)S(1)}, u32[]{:S(2)}, u32[]{:S(2)}) %collective-permute-start.1) | collective-permute-done | bytes 36896 | tf_op jit(solution)/shard_map/ppermute | solution.py:305
  10.7 1.4 %collective-permute-done.2.refs_3_ = f32[72,128]{1,0:T(8,128)S(1)} collective-permute-done((f32[72,128]{1,0:T(8,128)S(1)}, f32[72,128]{1,0:T(8,128)S(1)}, u32[]{:S(2)}, u32[]{:S(2)}) %collective-permute-start.2) | collective-permute-done | bytes 36896 | tf_op jit(solution)/shard_map/ppermute | solution.py:305
  12.1 3.7 %collective-permute-start.5 = (f32[72,128]{1,0:T(8,128)S(1)}, f32[72,128]{1,0:T(8,128)S(1)}, u32[]{:S(2)}, u32[]{:S(2)}) collective-permute-start(f32[72,128]{1,0:T(8,128)S(1)} %shard_map.97.refs_0_), channel_id=1, source_target_pairs={{0,12},{1,13},{2,14},{3,15},{4,8},{5,9},{6,10},{7,11},{8,4},{9,5},... | collective-permute-start | bytes 110600 | tf_op jit(solution)/shard_map/ppermute | solution.py:305
  15.8 0.0 collective-permute-start.4
  15.8 0.8 collective-permute-start.3
  16.6 1.4 %collective-permute-done.5.refs_3_ = f32[72,128]{1,0:T(8,128)S(1)} collective-permute-done((f32[72,128]{1,0:T(8,128)S(1)}, f32[72,128]{1,0:T(8,128)S(1)}, u32[]{:S(2)}, u32[]{:S(2)}) %collective-permute-start.5) | collective-permute-done | bytes 36896 | tf_op jit(solution)/shard_map/ppermute | solution.py:305
  17.9 2.7 %collective-permute-done.4.refs_2_ = f32[72,128]{1,0:T(8,128)S(1)} collective-permute-done((f32[72,128]{1,0:T(8,128)S(1)}, f32[72,128]{1,0:T(8,128)S(1)}, u32[]{:S(2)}, u32[]{:S(2)}) %collective-permute-start.4) | collective-permute-done | bytes 36896 | tf_op jit(solution)/shard_map/ppermute | solution.py:305
  20.6 0.0 collective-permute-done.3.refs_1_
  20.7 0.1 collective-permute-start.8
  20.7 0.9 collective-permute-start.7
  21.7 0.9 collective-permute-start.6
  22.6 0.0 copy-done.6
  22.6 2.3 %shard_map.96 = (f32[15,2,128,128]{3,2,1,0:T(8,128)S(1)}, f32[8,128]{1,0:T(8,128)S(1)}) custom-call(s32[2,15]{1,0:T(2,128)S(1)} %bitcast.15, f32[128,2,8,128]{3,2,1,0:T(8,128)S(1)} %get-tuple-element.17.obj), custom_call_target="tpu_custom_call" | custom-call | flops 2621440 | bytes 3018872 | tf_op jit(solution)/shard_map/pallas_call | solution.py:278
  24.8 0.0 collective-permute-done.8.refs_3_
  24.9 0.2 collective-permute-done.7.refs_2_
  25.1 0.0 collective-permute-done.6.refs_1_
  25.1 0.0 copy-done.2
  25.1 0.0 copy-done.3
  25.1 0.0 copy-done.4
  25.1 0.0 copy-done.5
  25.1 0.0 copy-start.7
  25.1 2.8 %shard_map.99 = (f32[2,128,128]{2,1,0:T(8,128)S(1)}, f32[128,2,8,128]{3,2,1,0:T(8,128)S(1)}, f32[72,128]{1,0:T(8,128)S(1)}, f32[72,128]{1,0:T(8,128)S(1)}, f32[72,128]{1,0:T(8,128)S(1)}, /*index=5*/f32[72,128]{1,0:T(8,128)S(1)}) custom-call(s32[1]{0:T(128)} %bitcast.low, s32[2,15]{1,0:T(2,128)S(1)} %bitcast.16, ...), custom_call_target="tpu_custom_call" | custom-call | flops 1006632960 | bytes 5378172 | tf_op jit(solution)/shard_map/pallas_call | solution.py:278
  27.9 28.0 %all_to_all.10 = f32[128,2,8,128]{3,2,1,0:T(8,128)S(1)} all-to-all(f32[128,2,8,128]{3,2,1,0:T(8,128)S(1)} %get-tuple-element.24), channel_id=1, replica_groups=mesh['scan'=2,'angle'=16] {'angle'}, dimensions={0} | all-to-all | bytes 2097152 | tf_op jit(solution)/shard_map/all_to_all | solution.py:358
  56.0 0.0 copy-done.7
  56.0 2.0 %shard_map.100 = f32[16,8,2,8,128]{4,3,2,1,0:T(8,128)} custom-call(s32[16]{0:T(128)S(1)} %copy-done.7, f32[16,8,2,8,128]{4,3,2,1,0:T(8,128)S(1)} %bitcast.10), custom_call_target="tpu_custom_call" | custom-call | flops 2621440 | bytes 2097216 | tf_op jit(solution)/shard_map/pallas_call | solution.py:278
  58.0 5.0 %all-to-all-start.1 = ((f32[128,2,8,128]{3,2,1,0:T(8,128)}), f32[128,2,8,128]{3,2,1,0:T(8,128)S(1)}, u32[]{:S(2)}, u32[]{:S(2)}) async-start(f32[128,2,8,128]{3,2,1,0:T(8,128)} %bitcast.7), calls=%async_computation.1 | async-start | bytes 2097152 | tf_op jit(solution)/shard_map/all_to_all | solution.py:358
  63.0 0.4 collective-permute-start.9
  63.4 1.6 %collective-permute-start.10 = (f32[72,128]{1,0:T(8,128)S(1)}, f32[72,128]{1,0:T(8,128)S(1)}, u32[]{:S(2)}, u32[]{:S(2)}) collective-permute-start(f32[72,128]{1,0:T(8,128)S(1)} %get-tuple-element.30), channel_id=1, source_target_pairs={{0,2},{1,3},{2,0},{3,1},{4,6},{5,7},{6,4},{7,5},{8,10},{9,11},{10,... | collective-permute-start | bytes 110600 | tf_op jit(solution)/shard_map/ppermute | solution.py:305
  65.1 0.0 collective-permute-start.11
  65.1 0.0 collective-permute-done.9.refs_1_
  65.1 8.4 %collective-permute-done.10.refs_2_ = f32[72,128]{1,0:T(8,128)S(1)} collective-permute-done((f32[72,128]{1,0:T(8,128)S(1)}, f32[72,128]{1,0:T(8,128)S(1)}, u32[]{:S(2)}, u32[]{:S(2)}) %collective-permute-start.10) | collective-permute-done | bytes 36896 | tf_op jit(solution)/shard_map/ppermute | solution.py:305
  73.4 0.0 collective-permute-done.11.refs_3_
  73.4 4.0 %collective-permute-start.14 = (f32[72,128]{1,0:T(8,128)S(1)}, f32[72,128]{1,0:T(8,128)S(1)}, u32[]{:S(2)}, u32[]{:S(2)}) collective-permute-start(f32[72,128]{1,0:T(8,128)S(1)} %shard_map.103.refs_0_), channel_id=1, source_target_pairs={{0,12},{1,13},{2,14},{3,15},{4,8},{5,9},{6,10},{7,11},{8,4},{9,5},... | collective-permute-start | bytes 110600 | tf_op jit(solution)/shard_map/ppermute | solution.py:305
  77.4 0.0 collective-permute-start.13
  77.4 0.6 collective-permute-start.12
  78.1 8.2 %collective-permute-done.14.refs_3_ = f32[72,128]{1,0:T(8,128)S(1)} collective-permute-done((f32[72,128]{1,0:T(8,128)S(1)}, f32[72,128]{1,0:T(8,128)S(1)}, u32[]{:S(2)}, u32[]{:S(2)}) %collective-permute-start.14) | collective-permute-done | bytes 36896 | tf_op jit(solution)/shard_map/ppermute | solution.py:305
  86.3 6.4 %collective-permute-done.13.refs_2_ = f32[72,128]{1,0:T(8,128)S(1)} collective-permute-done((f32[72,128]{1,0:T(8,128)S(1)}, f32[72,128]{1,0:T(8,128)S(1)}, u32[]{:S(2)}, u32[]{:S(2)}) %collective-permute-start.13) | collective-permute-done | bytes 36896 | tf_op jit(solution)/shard_map/ppermute | solution.py:305
  92.7 0.0 collective-permute-done.12.refs_1_
  92.7 0.4 collective-permute-start.17
  93.1 1.2 %collective-permute-start.16 = (f32[72,128]{1,0:T(8,128)S(1)}, f32[72,128]{1,0:T(8,128)S(1)}, u32[]{:S(2)}, u32[]{:S(2)}) collective-permute-start(f32[72,128]{1,0:T(8,128)S(1)} %shard_map.104.refs_0_), channel_id=1, source_target_pairs={{0,2},{1,3},{2,0},{3,1},{4,6},{5,7},{6,4},{7,5},{8,10},{9,11},{10,... | collective-permute-start | bytes 110600 | tf_op jit(solution)/shard_map/ppermute | solution.py:305
  94.3 0.3 collective-permute-start.15
  94.6 0.0 copy-start
  94.6 2.2 %copy-done = f32[1,1024,1024]{2,1,0:T(8,128)S(1)} copy-done((f32[1,1024,1024]{2,1,0:T(8,128)S(1)}, f32[1,1024,1024]{2,1,0:T(8,128)}, u32[]{:S(2)}) %copy-start) | copy-done | bytes 4194328
  96.8 0.7 shard_map.101
  97.5 0.0 copy-start.1
  97.5 1.3 %copy-done.1 = bf16[1024,1024]{1,0:T(8,128)(2,1)} copy-done((bf16[1024,1024]{1,0:T(8,128)(2,1)}, bf16[1024,1024]{1,0:T(8,128)(2,1)S(1)}, u32[]{:S(2)}) %copy-start.1) | copy-done | bytes 2097176
  98.9 0.0 collective-permute-done.17.refs_3_
  98.9 0.0 collective-permute-done.16.refs_2_
  98.9 0.0 collective-permute-done.15.refs_1_
  98.9 0.8 shard_map.105
  99.7 0.0 all-to-all-done.1.harm
  99.7 3.8 %shard_map.102 = f32[2,128,1024]{2,1,0:T(8,128)} custom-call(f32[128,2,8,128]{3,2,1,0:T(8,128)S(1)} %all-to-all-done.1.harm, bf16[1024,1024]{1,0:T(8,128)(2,1)S(1)} %get-tuple-element.25.r_high, bf16[1024,1024]{1,0:T(8,128)(2,1)} %copy-done.1), custom_call_target="tpu_custom_call" | custom-call | flops 1610612736 | bytes 6291456 | tf_op jit(solution)/shard_map/pallas_call | solution.py:278
  (4 shorter events, 0.1 us)
Async XLA Ops:
  0.6 21.9 %copy-start.6 = (s32[1,15,2]{1,2,0:T(2,128)S(1)}, s32[1,15,2]{1,2,0:T(2,128)}, u32[]{:S(2)}) copy-start(s32[1,15,2]{1,2,0:T(2,128)} %param.10) | copy-start | bytes 364
  0.6 24.4 %copy-start.2 = (bf16[1,15,128,128]{3,2,1,0:T(8,128)(2,1)S(1)}, bf16[1,15,128,128]{3,2,1,0:T(8,128)(2,1)}, u32[]{:S(2)}) copy-start(bf16[1,15,128,128]{3,2,1,0:T(8,128)(2,1)} %param.9) | copy-start | bytes 1474564
  0.7 24.4 %copy-start.3 = (f32[2,128,128]{2,1,0:T(8,128)S(1)}, f32[2,128,128]{2,1,0:T(8,128)}, u32[]{:S(2)}) copy-start(f32[2,128,128]{2,1,0:T(8,128)} %probe.1) | copy-start | bytes 393220
  0.7 24.4 %copy-start.4 = (bf16[256,256]{1,0:T(8,128)(2,1)S(1)}, bf16[256,256]{1,0:T(8,128)(2,1)}, u32[]{:S(2)}) copy-start(bf16[256,256]{1,0:T(8,128)(2,1)} %constant.11.clone.t2_far.t2) | copy-start | bytes 393220
  0.7 24.4 %copy-start.5 = (bf16[256,256]{1,0:T(8,128)(2,1)S(1)}, bf16[256,256]{1,0:T(8,128)(2,1)}, u32[]{:S(2)}) copy-start(bf16[256,256]{1,0:T(8,128)(2,1)} %constant.10.clone.t1_far.t1) | copy-start | bytes 393220
  5.5 3.1 %collective-permute-start = (f32[72,128]{1,0:T(8,128)S(1)}, f32[72,128]{1,0:T(8,128)S(1)}, u32[]{:S(2)}, u32[]{:S(2)}) collective-permute-start(f32[72,128]{1,0:T(8,128)S(1)} %get-tuple-element.21), channel_id=1, source_target_pairs={{0,1},{1,0},{2,3},{3,2},{4,5},{5,4},{6,7},{7,6},{8,9},{9,8},{10,11... | collective-permute-start | bytes 110600 | tf_op jit(solution)/shard_map/ppermute | solution.py:305
  6.1 4.6 %collective-permute-start.1 = (f32[72,128]{1,0:T(8,128)S(1)}, f32[72,128]{1,0:T(8,128)S(1)}, u32[]{:S(2)}, u32[]{:S(2)}) collective-permute-start(f32[72,128]{1,0:T(8,128)S(1)} %get-tuple-element.22), channel_id=1, source_target_pairs={{0,2},{1,3},{2,0},{3,1},{4,6},{5,7},{6,4},{7,5},{8,10},{9,11},{10,... | collective-permute-start | bytes 110600 | tf_op jit(solution)/shard_map/ppermute | solution.py:305
  8.6 3.4 %collective-permute-start.2 = (f32[72,128]{1,0:T(8,128)S(1)}, f32[72,128]{1,0:T(8,128)S(1)}, u32[]{:S(2)}, u32[]{:S(2)}) collective-permute-start(f32[72,128]{1,0:T(8,128)S(1)} %get-tuple-element.23), channel_id=1, source_target_pairs={{0,3},{1,2},{2,1},{3,0},{4,7},{5,6},{6,5},{7,4},{8,11},{9,10},{10,... | collective-permute-start | bytes 110600 | tf_op jit(solution)/shard_map/ppermute | solution.py:305
  12.1 5.8 %collective-permute-start.5 = (f32[72,128]{1,0:T(8,128)S(1)}, f32[72,128]{1,0:T(8,128)S(1)}, u32[]{:S(2)}, u32[]{:S(2)}) collective-permute-start(f32[72,128]{1,0:T(8,128)S(1)} %shard_map.97.refs_0_), channel_id=1, source_target_pairs={{0,12},{1,13},{2,14},{3,15},{4,8},{5,9},{6,10},{7,11},{8,4},{9,5},... | collective-permute-start | bytes 110600 | tf_op jit(solution)/shard_map/ppermute | solution.py:305
  15.8 4.9 %collective-permute-start.4 = (f32[72,128]{1,0:T(8,128)S(1)}, f32[72,128]{1,0:T(8,128)S(1)}, u32[]{:S(2)}, u32[]{:S(2)}) collective-permute-start(f32[72,128]{1,0:T(8,128)S(1)} %shard_map.97.refs_0_), channel_id=1, source_target_pairs={{0,8},{1,9},{2,10},{3,11},{4,12},{5,13},{6,14},{7,15},{8,0},{9,1},... | collective-permute-start | bytes 110600 | tf_op jit(solution)/shard_map/ppermute | solution.py:305
  15.8 4.9 %collective-permute-start.3 = (f32[72,128]{1,0:T(8,128)S(1)}, f32[72,128]{1,0:T(8,128)S(1)}, u32[]{:S(2)}, u32[]{:S(2)}) collective-permute-start(f32[72,128]{1,0:T(8,128)S(1)} %shard_map.97.refs_0_), channel_id=1, source_target_pairs={{0,4},{1,5},{2,6},{3,7},{4,0},{5,1},{6,2},{7,3},{8,12},{9,13},{10,... | collective-permute-start | bytes 110600 | tf_op jit(solution)/shard_map/ppermute | solution.py:305
  20.7 4.2 %collective-permute-start.8 = (f32[72,128]{1,0:T(8,128)S(1)}, f32[72,128]{1,0:T(8,128)S(1)}, u32[]{:S(2)}, u32[]{:S(2)}) collective-permute-start(f32[72,128]{1,0:T(8,128)S(1)} %shard_map.98.refs_0_), channel_id=1, source_target_pairs={{0,3},{1,2},{2,1},{3,0},{4,7},{5,6},{6,5},{7,4},{8,11},{9,10},{10,... | collective-permute-start | bytes 110600 | tf_op jit(solution)/shard_map/ppermute | solution.py:305
  20.7 4.4 %collective-permute-start.7 = (f32[72,128]{1,0:T(8,128)S(1)}, f32[72,128]{1,0:T(8,128)S(1)}, u32[]{:S(2)}, u32[]{:S(2)}) collective-permute-start(f32[72,128]{1,0:T(8,128)S(1)} %shard_map.98.refs_0_), channel_id=1, source_target_pairs={{0,2},{1,3},{2,0},{3,1},{4,6},{5,7},{6,4},{7,5},{8,10},{9,11},{10,... | collective-permute-start | bytes 110600 | tf_op jit(solution)/shard_map/ppermute | solution.py:305
  21.7 3.4 %collective-permute-start.6 = (f32[72,128]{1,0:T(8,128)S(1)}, f32[72,128]{1,0:T(8,128)S(1)}, u32[]{:S(2)}, u32[]{:S(2)}) collective-permute-start(f32[72,128]{1,0:T(8,128)S(1)} %shard_map.98.refs_0_), channel_id=1, source_target_pairs={{0,1},{1,0},{2,3},{3,2},{4,5},{5,4},{6,7},{7,6},{8,9},{9,8},{10,11... | collective-permute-start | bytes 110600 | tf_op jit(solution)/shard_map/ppermute | solution.py:305
  25.1 30.8 %copy-start.7 = (s32[16]{0:T(128)S(1)}, s32[16]{0:T(128)}, u32[]{:S(2)}) copy-start(s32[16]{0:T(128)} %angles.1) | copy-start | bytes 196
  58.0 41.7 %all-to-all-start.1 = ((f32[128,2,8,128]{3,2,1,0:T(8,128)}), f32[128,2,8,128]{3,2,1,0:T(8,128)S(1)}, u32[]{:S(2)}, u32[]{:S(2)}) async-start(f32[128,2,8,128]{3,2,1,0:T(8,128)} %bitcast.7), calls=%async_computation.1 | async-start | bytes 2097152 | tf_op jit(solution)/shard_map/all_to_all | solution.py:358
  63.0 2.0 %collective-permute-start.9 = (f32[72,128]{1,0:T(8,128)S(1)}, f32[72,128]{1,0:T(8,128)S(1)}, u32[]{:S(2)}, u32[]{:S(2)}) collective-permute-start(f32[72,128]{1,0:T(8,128)S(1)} %get-tuple-element.29), channel_id=1, source_target_pairs={{0,1},{1,0},{2,3},{3,2},{4,5},{5,4},{6,7},{7,6},{8,9},{9,8},{10,11... | collective-permute-start | bytes 110600 | tf_op jit(solution)/shard_map/ppermute | solution.py:305
  63.4 10.0 %collective-permute-start.10 = (f32[72,128]{1,0:T(8,128)S(1)}, f32[72,128]{1,0:T(8,128)S(1)}, u32[]{:S(2)}, u32[]{:S(2)}) collective-permute-start(f32[72,128]{1,0:T(8,128)S(1)} %get-tuple-element.30), channel_id=1, source_target_pairs={{0,2},{1,3},{2,0},{3,1},{4,6},{5,7},{6,4},{7,5},{8,10},{9,11},{10,... | collective-permute-start | bytes 110600 | tf_op jit(solution)/shard_map/ppermute | solution.py:305
  65.1 8.4 %collective-permute-start.11 = (f32[72,128]{1,0:T(8,128)S(1)}, f32[72,128]{1,0:T(8,128)S(1)}, u32[]{:S(2)}, u32[]{:S(2)}) collective-permute-start(f32[72,128]{1,0:T(8,128)S(1)} %get-tuple-element.31), channel_id=1, source_target_pairs={{0,3},{1,2},{2,1},{3,0},{4,7},{5,6},{6,5},{7,4},{8,11},{9,10},{10,... | collective-permute-start | bytes 110600 | tf_op jit(solution)/shard_map/ppermute | solution.py:305
  73.4 12.8 %collective-permute-start.14 = (f32[72,128]{1,0:T(8,128)S(1)}, f32[72,128]{1,0:T(8,128)S(1)}, u32[]{:S(2)}, u32[]{:S(2)}) collective-permute-start(f32[72,128]{1,0:T(8,128)S(1)} %shard_map.103.refs_0_), channel_id=1, source_target_pairs={{0,12},{1,13},{2,14},{3,15},{4,8},{5,9},{6,10},{7,11},{8,4},{9,5},... | collective-permute-start | bytes 110600 | tf_op jit(solution)/shard_map/ppermute | solution.py:305
  77.4 15.2 %collective-permute-start.13 = (f32[72,128]{1,0:T(8,128)S(1)}, f32[72,128]{1,0:T(8,128)S(1)}, u32[]{:S(2)}, u32[]{:S(2)}) collective-permute-start(f32[72,128]{1,0:T(8,128)S(1)} %shard_map.103.refs_0_), channel_id=1, source_target_pairs={{0,8},{1,9},{2,10},{3,11},{4,12},{5,13},{6,14},{7,15},{8,0},{9,1},... | collective-permute-start | bytes 110600 | tf_op jit(solution)/shard_map/ppermute | solution.py:305
  77.4 15.2 %collective-permute-start.12 = (f32[72,128]{1,0:T(8,128)S(1)}, f32[72,128]{1,0:T(8,128)S(1)}, u32[]{:S(2)}, u32[]{:S(2)}) collective-permute-start(f32[72,128]{1,0:T(8,128)S(1)} %shard_map.103.refs_0_), channel_id=1, source_target_pairs={{0,4},{1,5},{2,6},{3,7},{4,0},{5,1},{6,2},{7,3},{8,12},{9,13},{10,... | collective-permute-start | bytes 110600 | tf_op jit(solution)/shard_map/ppermute | solution.py:305
  92.7 6.2 %collective-permute-start.17 = (f32[72,128]{1,0:T(8,128)S(1)}, f32[72,128]{1,0:T(8,128)S(1)}, u32[]{:S(2)}, u32[]{:S(2)}) collective-permute-start(f32[72,128]{1,0:T(8,128)S(1)} %shard_map.104.refs_0_), channel_id=1, source_target_pairs={{0,3},{1,2},{2,1},{3,0},{4,7},{5,6},{6,5},{7,4},{8,11},{9,10},{10,... | collective-permute-start | bytes 110600 | tf_op jit(solution)/shard_map/ppermute | solution.py:305
  93.1 5.8 %collective-permute-start.16 = (f32[72,128]{1,0:T(8,128)S(1)}, f32[72,128]{1,0:T(8,128)S(1)}, u32[]{:S(2)}, u32[]{:S(2)}) collective-permute-start(f32[72,128]{1,0:T(8,128)S(1)} %shard_map.104.refs_0_), channel_id=1, source_target_pairs={{0,2},{1,3},{2,0},{3,1},{4,6},{5,7},{6,4},{7,5},{8,10},{9,11},{10,... | collective-permute-start | bytes 110600 | tf_op jit(solution)/shard_map/ppermute | solution.py:305
  94.3 4.6 %collective-permute-start.15 = (f32[72,128]{1,0:T(8,128)S(1)}, f32[72,128]{1,0:T(8,128)S(1)}, u32[]{:S(2)}, u32[]{:S(2)}) collective-permute-start(f32[72,128]{1,0:T(8,128)S(1)} %shard_map.104.refs_0_), channel_id=1, source_target_pairs={{0,1},{1,0},{2,3},{3,2},{4,5},{5,4},{6,7},{7,6},{8,9},{9,8},{10,11... | collective-permute-start | bytes 110600 | tf_op jit(solution)/shard_map/ppermute | solution.py:305
  94.6 2.2 %copy-start = (f32[1,1024,1024]{2,1,0:T(8,128)S(1)}, f32[1,1024,1024]{2,1,0:T(8,128)}, u32[]{:S(2)}) copy-start(f32[1,1024,1024]{2,1,0:T(8,128)} %param.13) | copy-start | bytes 12582916
  97.5 1.3 %copy-start.1 = (bf16[1024,1024]{1,0:T(8,128)(2,1)}, bf16[1024,1024]{1,0:T(8,128)(2,1)S(1)}, u32[]{:S(2)}) copy-start(bf16[1024,1024]{1,0:T(8,128)(2,1)S(1)} %get-tuple-element.26.r_low_far) | copy-start | bytes 6291460
where the time goes:
time: 104 us; the launch traced here: 103 us
  waiting for transfers between devices  30.7 us (30%)
  blocking collectives  28 us (27%)
  starting transfers between devices  23.1 us (22%)
  Pallas kernels  17.3 us (17%)
  local copies, waits for them, and re-layouts  3.56 us (3%)
    ppermute x18, waiting for transfers between devices, swap(): return lax.ppermute(x, axis, [(i, i ^ mask) for i in range(count)])  30.7 us
    all_to_all x1, blocking collectives, exchange(): return lax.all_to_all(x, 'angle', split_axis=0, concat_axis=0, tiled=True)  28 us
    ppermute x18, starting transfers between devices, swap(): return lax.ppermute(x, axis, [(i, i ^ mask) for i in range(count)])  18.1 us
    pallas_call x11, Pallas kernels, call(): pl.pallas_call(kernel, out_shape=out_shape, in_specs=specs, out_specs=jax...  17.3 us
    all_to_all x1, starting transfers between devices, exchange(): return lax.all_to_all(x, 'angle', split_axis=0, concat_axis=0, tiled=True)  5.02 us
    unnamed x16, local copies, waits for them, and re-layouts  3.56 us
  transfers between devices with their start and end apart: 19, of which 8 were waited for; matrix products, arithmetic and copies ran while one was open for 0% of the time, Pallas kernels for 4%

commit v1 on v0

--- a/solution.py
+++ b/solution.py
@@ -89,8 +89,9 @@
         mask = lane >= rem
         for c, value in ((0, step_re * gr + step_im * gi), (1, step_re * gi - step_im * gr)):
             r = pltpu.roll(value, lax.rem(rem, LANES), 1)
-            for t, part in ((q, jnp.where(mask, r, 0.0)), (q + 1, jnp.where(mask, 0.0, r))):
-                view[:, t, c] = view[:, t, c] - part.reshape(size // SUBLANES, SUBLANES, LANES)
+            r = r.reshape(size // SUBLANES, SUBLANES, LANES)
+            for t, own in ((q, mask), (q + 1, ~mask)):
+                pltpu.store(view.at[:, t, c], view[:, t, c] - r, mask=own.reshape(r.shape))
     pg[:size] = total_re
     pg[size : 2 * size] = total_im
 
@@ -106,7 +107,7 @@
 def hand_out(low, pg, parts):
     height = parts[0].shape[0] - SUBLANES
     for m, part in enumerate(parts):
-        start = pl.multiple_of((low[0] ^ m) * height, SUBLANES)
+        start = pl.multiple_of((low[0] & (len(parts) - 1) ^ m) * height, SUBLANES)
         part[:height] = pg[pl.ds(start, height)]
         part[height:] = pg[height * len(parts) :]
 
@@ -118,7 +119,7 @@
     share = min(height, size)
     for m, block in enumerate(blocks):
         for piece in range(height // share):
-            start = (low[0] ^ m) * height + piece * share
+            start = (low[0] & (len(blocks) - 1) ^ m) * height + piece * share
             where = (start // size, pl.ds(pl.multiple_of(start % size, SUBLANES), share))
             gradient = block[piece * share : piece * share + share]
             out[where] = probe[where] - probe_rate * gradient / energy
@@ -179,7 +180,7 @@
 
 
 def second_kernel(inner, low, pos, obj, pieces, energy, measured, probe, t1, t2, *refs):
-    blocks, (prb_out, out), parts, pg = refs[:inner], refs[inner : inner + 2], refs[inner + 2 : -1], refs[-1]
+    blocks, prb_out, out, parts, pg = refs[:inner], refs[inner], refs[inner + 1], refs[inner + 2 : -1], refs[-1]
     size = probe.shape[1]
     collect(low, blocks, probe, prb_out)
     pg[2 * size :] = energy[...]
@@ -216,8 +217,8 @@
     return low + high
 
 
-def angular_kernel(angles, blocks, out, where):
-    count = blocks.shape[0]
+def angular_kernel(angles, blocks, far, where, out, sem):
+    count, share = blocks.shape[:2]
 
     def note(b, carry):
         where[angles[b]] = b
@@ -225,8 +226,8 @@
 
     lax.fori_loop(0, count, note, 0)
     scale = 1.0 / math.sqrt(count)
-
-    def cell(j, carry):
+    copies = []
+    for j in range(share):
         values = []
         for a in range(count):
             block = blocks[where[a], j]
@@ -234,9 +235,10 @@
         for k, (re, im) in enumerate(butterfly(values)):
             out[k, j, 0] = re
             out[k, j, 1] = im
-        return carry
-
-    lax.fori_loop(0, blocks.shape[1], cell, 0)
+        copies.append(pltpu.make_async_copy(out.at[:, j], far.at[:, j], sem.at[j]))
+        copies[-1].start()
+    for copy in copies:
+        copy.wait()
 
 
 def split(x):
@@ -248,26 +250,40 @@
     high[...], low[...] = split(radial[...])
 
 
-def invert_kernel(harm, r_high, r_low_far, out, x_high, x_low, r_low, sem):
-    copy = pltpu.make_async_copy(r_low_far, r_low, sem)
+def invert_kernel(harm, r_high, r_low_far, far, x, r_low, out, sem):
+    copy = pltpu.make_async_copy(r_low_far, r_low, sem.at[0])
     copy.start()
     cells, _, rows, lanes = harm.shape
-    tiles = r_high.shape[0] // lanes
+    columns = r_high.shape[0]
+    tiles = columns // lanes
     height = cells // tiles * rows
     for r in range(cells // tiles):
         for t in range(tiles):
             for c in range(2):
-                where = (slice(c * height + r * 8, c * height + r * 8 + 8), slice(t * 128, t * 128 + 128))
-                x_high[where], x_low[where] = split(harm[r * tiles + t, c])
-    value = dot(x_high[...], r_high[...]) + dot(x_low[...], r_high[...])
-    copy.wait()
-    out[...] = (value + dot(x_high[...], r_low[...])).reshape(out.shape)
-
-
+                high, low = split(harm[r * tiles + t, c])
+                start = c * height + r * rows
+                x[start : start + rows, t * lanes : t * lanes + lanes] = high
+                x[2 * height + start : 2 * height + start + rows, t * lanes : t * lanes + lanes] = low
+    span = columns // SPANS
+    copies = []
+    for i in range(SPANS):
+        inside = slice(i * span, i * span + span)
+        value = dot(x[...], r_high[:, inside])
+        if i == 0:
+            copy.wait()
+        value = value[: 2 * height] + value[2 * height :] + dot(x[: 2 * height], r_low[:, inside])
+        out[:, :, inside] = value.reshape(2, height, span)
+        copies.append(pltpu.make_async_copy(out.at[:, :, inside], far.at[:, :, inside], sem.at[i + 1]))
+        copies[-1].start()
+    for copy in copies:
+        copy.wait()
+
+
+SPANS = 2
 HBM = pltpu.MemorySpace.HBM
 
 
-def call(kernel, out_shape, args, scratch=(), flops=0, scalars=0, far=(), limit=2):
+def call(kernel, out_shape, args, scratch=(), flops=0, scalars=0, far=(), limit=2, far_out=False):
     moved = sum(math.prod(x.shape) * x.dtype.itemsize for x in (*args, *jax.tree.leaves(out_shape)))
     specs = [SMEM] * scalars + [VMEM] * (len(args) - scalars)
     args = list(args)
@@ -279,7 +295,7 @@
         kernel,
         out_shape=out_shape,
         in_specs=specs,
-        out_specs=jax.tree.map(lambda _: VMEM, out_shape),
+        out_specs=jax.tree.map(lambda _: pl.BlockSpec(memory_space=pl.ANY) if far_out else VMEM, out_shape),
         scratch_shapes=scratch,
         cost_estimate=pl.CostEstimate(flops=flops, bytes_accessed=moved, transcendentals=0),
         compiler_params=pltpu.CompilerParams(vmem_limit_bytes=limit << 20),
@@ -322,9 +338,11 @@
     t1, t2 = transform_tables(size)
     obj, meas, pos = object_init[0], measured[0], positions[0].T
     flops = patches * 4 * 2 * (2 * size) * (2 * size) * size
-    inner = 1 << (count.bit_length() // 2)
-    low = (lax.axis_index("angle") & (inner - 1)).reshape(1)
+    bits = count.bit_length() - 1
+    inner, late = 1 << bits // 2, 1 << (bits + 2) // 2
+    low = lax.axis_index("angle").reshape(1)
     messages = [shape((2 * size // inner + SUBLANES, LANES), f32)] * inner
+    late_messages = [shape((2 * size // late + SUBLANES, LANES), f32)] * late
     field = shape((cells, 2, SUBLANES, LANES), f32)
     windows = (patches, 2, size, LANES)
     gradient = pltpu.VMEM((2 * size + SUBLANES, LANES), f32)
@@ -346,7 +364,7 @@
     blocks = all_sum(parts, "angle", count)
     prb, obj, *parts = call(
         functools.partial(second_kernel, inner),
-        [shape(probe.shape, f32), field, *messages],
+        [shape(probe.shape, f32), field, *late_messages],
         (low, pos, obj, pieces, energy, meas, probe, t1, t2, *blocks),
         [gradient],
         flops,
@@ -363,22 +381,32 @@
         angular_kernel,
         grouped,
         (angle_list, received.reshape(grouped.shape)),
-        [pltpu.SMEM((count,), jnp.int32)],
+        [
+            pltpu.SMEM((count,), jnp.int32),
+            pltpu.VMEM(grouped.shape, f32),
+            pltpu.SemaphoreType.DMA((cells // count,)),
+        ],
         10 * received.size,
         1,
         limit=8,
+        far_out=True,
     ).reshape(field.shape)
     harm = exchange(harm)
     slices = call(
         invert_kernel,
         shape(object_init.shape[1:], f32),
         (harm, r_high, r_low),
-        [pltpu.VMEM((2 * rows, columns), bf16)] * 2
-        + [pltpu.VMEM(r_low.shape, bf16), pltpu.SemaphoreType.DMA],
+        [
+            pltpu.VMEM((4 * rows, columns), bf16),
+            pltpu.VMEM(r_low.shape, bf16),
+            pltpu.VMEM(object_init.shape[1:], f32),
+            pltpu.SemaphoreType.DMA((SPANS + 1,)),
+        ],
         6 * 2 * rows * columns * columns,
         0,
         far=(2,),
         limit=12,
+        far_out=True,
     )
     blocks = all_sum(parts, "angle", count)
     probe_out = call(probe_kernel, shape(probe.shape, f32), (low, prb, *blocks), scalars=1)

time: 104 us -> 106 us (1.019)
  starting transfers between devices: 23.1 us -> 32.4 us
  waiting for transfers between devices: 30.7 us -> 23.5 us
    ppermute x18 -> x24, starting transfers between devices: 18.1 us -> 27.3 us  [swap(): return lax.ppermute(x, axis, [(i, i ^ mask) for i in range(count)])]
    ppermute x18 -> x24, waiting for transfers between devices: 30.7 us -> 23.5 us  [swap(): return lax.ppermute(x, axis, [(i, i ^ mask) for i in range(count)])]
  transfers between devices with their start and end apart: 19 -> 25, of which waited for: 8 -> 11; matrix products, arithmetic and copies ran while one was open for 0% -> 0% of each run, Pallas kernels for 4% -> 4%
where the time goes in v1:
time: 106 us; the launch traced here: 105 us
  starting transfers between devices  32.4 us (31%)
  blocking collectives  28 us (26%)
  waiting for transfers between devices  23.5 us (22%)
  Pallas kernels  17.2 us (16%)
  local copies, waits for them, and re-layouts  3.57 us (3%)
    all_to_all x1, blocking collectives, exchange(): return lax.all_to_all(x, 'angle', split_axis=0, concat_axis=0, tiled=True)  28 us
    ppermute x24, starting transfers between devices, swap(): return lax.ppermute(x, axis, [(i, i ^ mask) for i in range(count)])  27.3 us
    ppermute x24, waiting for transfers between devices, swap(): return lax.ppermute(x, axis, [(i, i ^ mask) for i in range(count)])  23.5 us
    pallas_call x11, Pallas kernels, call(): pl.pallas_call(kernel, out_shape=out_shape, in_specs=specs, out_specs=jax...  17.2 us
    all_to_all x1, starting transfers between devices, exchange(): return lax.all_to_all(x, 'angle', split_axis=0, concat_axis=0, tiled=True)  5.04 us
    unnamed x16, local copies, waits for them, and re-layouts  3.57 us
  transfers between devices with their start and end apart: 25, of which 11 were waited for; matrix products, arithmetic and copies ran while one was open for 0% of the time, Pallas kernels for 4%

profile of v1, /device:TPU:0, one launch (start us, length us, event | category | flops | bytes accessed | tf_op | source)
XLA Modules:
  0.0 105.5 jit_solution(10487559001964063071)
XLA Ops:
  0.6 0.0 copy-start.6
  0.7 0.0 copy-start.4
  0.7 0.0 copy-start.5
  0.7 4.8 %shard_map.95 = (f32[128,2,8,128]{3,2,1,0:T(8,128)S(1)}, f32[72,128]{1,0:T(8,128)S(1)}, f32[72,128]{1,0:T(8,128)S(1)}, f32[72,128]{1,0:T(8,128)S(1)}, f32[72,128]{1,0:T(8,128)S(1)}) custom-call(s32[1]{0:T(128)} %bitcast.low, s32[2,15]{1,0:T(2,128)} %bitcast.14, f32[2,128,1024]{2,1,0:T(8,128)} %bitcast.18, bf16[15,128,128]{2,1,0:T(8,128)(2,1)} %bitcast.12, ...), custom_call_target="tpu_custom_call" | custom-call | flops 1006632960 | bytes 3129468 | tf_op jit(solution)/shard_map/pallas_call | solution.py:294
  5.5 0.6 collective-permute-start
  6.0 2.6 %collective-permute-start.1 = (f32[72,128]{1,0:T(8,128)S(1)}, f32[72,128]{1,0:T(8,128)S(1)}, u32[]{:S(2)}, u32[]{:S(2)}) collective-permute-start(f32[72,128]{1,0:T(8,128)S(1)} %get-tuple-element.26), channel_id=1, source_target_pairs={{0,2},{1,3},{2,0},{3,1},{4,6},{5,7},{6,4},{7,5},{8,10},{9,11},{10,... | collective-permute-start | bytes 110600 | tf_op jit(solution)/shard_map/ppermute | solution.py:321
  8.6 0.0 collective-permute-start.2
  8.6 0.0 collective-permute-done.refs_1_
  8.6 2.0 %collective-permute-done.1.refs_2_ = f32[72,128]{1,0:T(8,128)S(1)} collective-permute-done((f32[72,128]{1,0:T(8,128)S(1)}, f32[72,128]{1,0:T(8,128)S(1)}, u32[]{:S(2)}, u32[]{:S(2)}) %collective-permute-start.1) | collective-permute-done | bytes 36896 | tf_op jit(solution)/shard_map/ppermute | solution.py:321
  10.6 1.4 %collective-permute-done.2.refs_3_ = f32[72,128]{1,0:T(8,128)S(1)} collective-permute-done((f32[72,128]{1,0:T(8,128)S(1)}, f32[72,128]{1,0:T(8,128)S(1)}, u32[]{:S(2)}, u32[]{:S(2)}) %collective-permute-start.2) | collective-permute-done | bytes 36896 | tf_op jit(solution)/shard_map/ppermute | solution.py:321
  12.0 3.7 %collective-permute-start.5 = (f32[72,128]{1,0:T(8,128)S(1)}, f32[72,128]{1,0:T(8,128)S(1)}, u32[]{:S(2)}, u32[]{:S(2)}) collective-permute-start(f32[72,128]{1,0:T(8,128)S(1)} %shard_map.97.refs_0_), channel_id=1, source_target_pairs={{0,12},{1,13},{2,14},{3,15},{4,8},{5,9},{6,10},{7,11},{8,4},{9,5},... | collective-permute-start | bytes 110600 | tf_op jit(solution)/shard_map/ppermute | solution.py:321
  15.7 0.0 collective-permute-start.4
  15.7 0.8 collective-permute-start.3
  16.5 1.4 %collective-permute-done.5.refs_3_ = f32[72,128]{1,0:T(8,128)S(1)} collective-permute-done((f32[72,128]{1,0:T(8,128)S(1)}, f32[72,128]{1,0:T(8,128)S(1)}, u32[]{:S(2)}, u32[]{:S(2)}) %collective-permute-start.5) | collective-permute-done | bytes 36896 | tf_op jit(solution)/shard_map/ppermute | solution.py:321
  17.8 2.7 %collective-permute-done.4.refs_2_ = f32[72,128]{1,0:T(8,128)S(1)} collective-permute-done((f32[72,128]{1,0:T(8,128)S(1)}, f32[72,128]{1,0:T(8,128)S(1)}, u32[]{:S(2)}, u32[]{:S(2)}) %collective-permute-start.4) | collective-permute-done | bytes 36896 | tf_op jit(solution)/shard_map/ppermute | solution.py:321
  20.5 0.0 collective-permute-done.3.refs_1_
  20.6 0.1 collective-permute-start.8
  20.6 0.9 collective-permute-start.7
  21.6 0.9 collective-permute-start.6
  22.5 2.3 %shard_map.96 = (f32[15,2,128,128]{3,2,1,0:T(8,128)S(1)}, f32[8,128]{1,0:T(8,128)S(1)}) custom-call(s32[2,15]{1,0:T(2,128)S(1)} %bitcast.15, f32[128,2,8,128]{3,2,1,0:T(8,128)S(1)} %get-tuple-element.21.obj), custom_call_target="tpu_custom_call" | custom-call | flops 2621440 | bytes 3018872 | tf_op jit(solution)/shard_map/pallas_call | solution.py:294
  24.8 0.0 collective-permute-done.8.refs_3_
  24.8 0.2 collective-permute-done.7.refs_2_
  25.0 0.0 collective-permute-done.6.refs_1_
  25.0 0.0 copy-start.7
  25.0 2.7 %shard_map.99 = (f32[2,128,128]{2,1,0:T(8,128)S(1)}, f32[128,2,8,128]{3,2,1,0:T(8,128)S(1)}, f32[40,128]{1,0:T(8,128)S(1)}, f32[40,128]{1,0:T(8,128)S(1)}, f32[4...) custom-call(s32[1]{0:T(128)} %bitcast.low, ...), custom_call_target="tpu_custom_call" | custom-call | flops 1006632960 | bytes 5394556 | tf_op jit(solution)/shard_map/pallas_call | solution.py:294
  27.8 28.0 %all_to_all.10 = f32[128,2,8,128]{3,2,1,0:T(8,128)S(1)} all-to-all(f32[128,2,8,128]{3,2,1,0:T(8,128)S(1)} %get-tuple-element.28), channel_id=1, replica_groups=mesh['scan'=2,'angle'=16] {'angle'}, dimensions={0} | all-to-all | bytes 2097152 | tf_op jit(solution)/shard_map/all_to_all | solution.py:376
  55.8 1.8 %shard_map.100 = f32[16,8,2,8,128]{4,3,2,1,0:T(8,128)} custom-call(s32[16]{0:T(128)S(1)} %copy-done.7, f32[16,8,2,8,128]{4,3,2,1,0:T(8,128)S(1)} %bitcast.10), custom_call_target="tpu_custom_call" | custom-call | flops 2621440 | bytes 2097216 | tf_op jit(solution)/shard_map/pallas_call | solution.py:294
  57.6 5.0 %all-to-all-start.1 = ((f32[128,2,8,128]{3,2,1,0:T(8,128)}), f32[128,2,8,128]{3,2,1,0:T(8,128)S(1)}, u32[]{:S(2)}, u32[]{:S(2)}) async-start(f32[128,2,8,128]{3,2,1,0:T(8,128)} %bitcast.7), calls=%async_computation.1 | async-start | bytes 2097152 | tf_op jit(solution)/shard_map/all_to_all | solution.py:376
  62.6 0.4 collective-permute-start.9
  63.0 1.6 %collective-permute-start.10 = (f32[40,128]{1,0:T(8,128)S(1)}, f32[40,128]{1,0:T(8,128)S(1)}, u32[]{:S(2)}, u32[]{:S(2)}) collective-permute-start(f32[40,128]{1,0:T(8,128)S(1)} %get-tuple-element.34), channel_id=1, source_target_pairs={{0,2},{1,3},{2,0},{3,1},{4,6},{5,7},{6,4},{7,5},{8,10},{9,11},{10,... | collective-permute-start | bytes 61448 | tf_op jit(solution)/shard_map/ppermute | solution.py:321
  64.7 0.0 collective-permute-start.11
  64.7 1.7 %collective-permute-start.12 = (f32[40,128]{1,0:T(8,128)S(1)}, f32[40,128]{1,0:T(8,128)S(1)}, u32[]{:S(2)}, u32[]{:S(2)}) collective-permute-start(f32[40,128]{1,0:T(8,128)S(1)} %get-tuple-element.36), channel_id=1, source_target_pairs={{0,4},{1,5},{2,6},{3,7},{4,0},{5,1},{6,2},{7,3},{8,12},{9,13},{10,... | collective-permute-start | bytes 61448 | tf_op jit(solution)/shard_map/ppermute | solution.py:321
  66.4 0.1 collective-permute-start.13
  66.5 0.0 collective-permute-done.9.refs_1_
  66.5 2.5 %collective-permute-start.14 = (f32[40,128]{1,0:T(8,128)S(1)}, f32[40,128]{1,0:T(8,128)S(1)}, u32[]{:S(2)}, u32[]{:S(2)}) collective-permute-start(f32[40,128]{1,0:T(8,128)S(1)} %get-tuple-element.38), channel_id=1, source_target_pairs={{0,6},{1,7},{2,4},{3,5},{4,2},{5,3},{6,0},{7,1},{8,14},{9,15},{10,... | collective-permute-start | bytes 61448 | tf_op jit(solution)/shard_map/ppermute | solution.py:321
  69.0 2.7 %collective-permute-done.10.refs_2_ = f32[40,128]{1,0:T(8,128)S(1)} collective-permute-done((f32[40,128]{1,0:T(8,128)S(1)}, f32[40,128]{1,0:T(8,128)S(1)}, u32[]{:S(2)}, u32[]{:S(2)}) %collective-permute-start.10) | collective-permute-done | bytes 20512 | tf_op jit(solution)/shard_map/ppermute | solution.py:321
  71.7 0.0 collective-permute-start.15
  71.7 0.0 collective-permute-done.11.refs_3_
  71.7 9.6 %collective-permute-done.12.refs_4_ = f32[40,128]{1,0:T(8,128)S(1)} collective-permute-done((f32[40,128]{1,0:T(8,128)S(1)}, f32[40,128]{1,0:T(8,128)S(1)}, u32[]{:S(2)}, u32[]{:S(2)}) %collective-permute-start.12) | collective-permute-done | bytes 20512 | tf_op jit(solution)/shard_map/ppermute | solution.py:321
  81.3 0.4 collective-permute-done.13.refs_5_
  81.8 0.4 collective-permute-done.14.refs_6_
  82.2 0.3 collective-permute-done.15.refs_7_
  82.5 5.1 %collective-permute-start.16 = (f32[40,128]{1,0:T(8,128)S(1)}, f32[40,128]{1,0:T(8,128)S(1)}, u32[]{:S(2)}, u32[]{:S(2)}) collective-permute-start(f32[40,128]{1,0:T(8,128)S(1)} %shard_map.103.refs_0_), channel_id=1, source_target_pairs={{0,8},{1,9},{2,10},{3,11},{4,12},{5,13},{6,14},{7,15},{8,0},{9,1},... | collective-permute-start | bytes 61448 | tf_op jit(solution)/shard_map/ppermute | solution.py:321
  87.6 2.4 %collective-permute-done.16.refs_1_ = f32[40,128]{1,0:T(8,128)S(1)} collective-permute-done((f32[40,128]{1,0:T(8,128)S(1)}, f32[40,128]{1,0:T(8,128)S(1)}, u32[]{:S(2)}, u32[]{:S(2)}) %collective-permute-start.16) | collective-permute-done | bytes 20512 | tf_op jit(solution)/shard_map/ppermute | solution.py:321
  90.0 0.0 collective-permute-start.23
  90.0 1.5 %collective-permute-start.22 = (f32[40,128]{1,0:T(8,128)S(1)}, f32[40,128]{1,0:T(8,128)S(1)}, u32[]{:S(2)}, u32[]{:S(2)}) collective-permute-start(f32[40,128]{1,0:T(8,128)S(1)} %shard_map.104.refs_0_), channel_id=1, source_target_pairs={{0,6},{1,7},{2,4},{3,5},{4,2},{5,3},{6,0},{7,1},{8,14},{9,15},{10,... | collective-permute-start | bytes 61448 | tf_op jit(solution)/shard_map/ppermute | solution.py:321
  91.6 1.3 %collective-permute-start.21 = (f32[40,128]{1,0:T(8,128)S(1)}, f32[40,128]{1,0:T(8,128)S(1)}, u32[]{:S(2)}, u32[]{:S(2)}) collective-permute-start(f32[40,128]{1,0:T(8,128)S(1)} %shard_map.104.refs_0_), channel_id=1, source_target_pairs={{0,5},{1,4},{2,7},{3,6},{4,1},{5,0},{6,3},{7,2},{8,13},{9,12},{10,... | collective-permute-start | bytes 61448 | tf_op jit(solution)/shard_map/ppermute | solution.py:321
  92.9 1.5 %collective-permute-start.20 = (f32[40,128]{1,0:T(8,128)S(1)}, f32[40,128]{1,0:T(8,128)S(1)}, u32[]{:S(2)}, u32[]{:S(2)}) collective-permute-start(f32[40,128]{1,0:T(8,128)S(1)} %shard_map.104.refs_0_), channel_id=1, source_target_pairs={{0,4},{1,5},{2,6},{3,7},{4,0},{5,1},{6,2},{7,3},{8,12},{9,13},{10,... | collective-permute-start | bytes 61448 | tf_op jit(solution)/shard_map/ppermute | solution.py:321
  94.4 0.3 collective-permute-start.19
  94.7 0.0 collective-permute-done.23.refs_7_
  94.7 1.2 %collective-permute-start.18 = (f32[40,128]{1,0:T(8,128)S(1)}, f32[40,128]{1,0:T(8,128)S(1)}, u32[]{:S(2)}, u32[]{:S(2)}) collective-permute-start(f32[40,128]{1,0:T(8,128)S(1)} %shard_map.104.refs_0_), channel_id=1, source_target_pairs={{0,2},{1,3},{2,0},{3,1},{4,6},{5,7},{6,4},{7,5},{8,10},{9,11},{10,... | collective-permute-start | bytes 61448 | tf_op jit(solution)/shard_map/ppermute | solution.py:321
  95.9 0.0 collective-permute-done.22.refs_6_
  95.9 0.4 collective-permute-start.17
  96.3 2.2 %copy-done = f32[1,1024,1024]{2,1,0:T(8,128)S(1)} copy-done((f32[1,1024,1024]{2,1,0:T(8,128)S(1)}, f32[1,1024,1024]{2,1,0:T(8,128)}, u32[]{:S(2)}) %copy-start) | copy-done | bytes 4194328
  98.5 0.7 shard_map.101
  99.2 1.3 %copy-done.1 = bf16[1024,1024]{1,0:T(8,128)(2,1)} copy-done((bf16[1024,1024]{1,0:T(8,128)(2,1)}, bf16[1024,1024]{1,0:T(8,128)(2,1)S(1)}, u32[]{:S(2)}) %copy-start.1) | copy-done | bytes 2097176
  100.5 0.0 collective-permute-done.21.refs_5_
  100.5 0.0 collective-permute-done.20.refs_4_
  100.5 0.0 collective-permute-done.19.refs_3_
  100.5 0.0 collective-permute-done.18.refs_2_
  100.5 0.0 collective-permute-done.17.refs_1_
  100.6 0.8 shard_map.105
  101.4 0.0 all-to-all-done.1.harm
  101.4 4.1 %shard_map.102 = f32[2,128,1024]{2,1,0:T(8,128)} custom-call(f32[128,2,8,128]{3,2,1,0:T(8,128)S(1)} %all-to-all-done.1.harm, bf16[1024,1024]{1,0:T(8,128)(2,1)S(1)} %get-tuple-element.29.r_high, bf16[1024,1024]{1,0:T(8,128)(2,1)} %copy-done.1), custom_call_target="tpu_custom_call" | custom-call | flops 1610612736 | bytes 6291456 | tf_op jit(solution)/shard_map/pallas_call | solution.py:294
  (14 shorter events, 0.1 us)
Async XLA Ops:
  0.6 21.9 %copy-start.6 = (s32[1,15,2]{1,2,0:T(2,128)S(1)}, s32[1,15,2]{1,2,0:T(2,128)}, u32[]{:S(2)}) copy-start(s32[1,15,2]{1,2,0:T(2,128)} %param.10) | copy-start | bytes 364
  0.6 24.4 %copy-start.2 = (bf16[1,15,128,128]{3,2,1,0:T(8,128)(2,1)S(1)}, bf16[1,15,128,128]{3,2,1,0:T(8,128)(2,1)}, u32[]{:S(2)}) copy-start(bf16[1,15,128,128]{3,2,1,0:T(8,128)(2,1)} %param.9) | copy-start | bytes 1474564
  0.7 24.4 %copy-start.3 = (f32[2,128,128]{2,1,0:T(8,128)S(1)}, f32[2,128,128]{2,1,0:T(8,128)}, u32[]{:S(2)}) copy-start(f32[2,128,128]{2,1,0:T(8,128)} %probe.1) | copy-start | bytes 393220
  0.7 24.3 %copy-start.4 = (bf16[256,256]{1,0:T(8,128)(2,1)S(1)}, bf16[256,256]{1,0:T(8,128)(2,1)}, u32[]{:S(2)}) copy-start(bf16[256,256]{1,0:T(8,128)(2,1)} %constant.9.clone.t2_far.t2) | copy-start | bytes 393220
  0.7 24.3 %copy-start.5 = (bf16[256,256]{1,0:T(8,128)(2,1)S(1)}, bf16[256,256]{1,0:T(8,128)(2,1)}, u32[]{:S(2)}) copy-start(bf16[256,256]{1,0:T(8,128)(2,1)} %constant.8.clone.t1_far.t1) | copy-start | bytes 393220
  5.5 3.2 %collective-permute-start = (f32[72,128]{1,0:T(8,128)S(1)}, f32[72,128]{1,0:T(8,128)S(1)}, u32[]{:S(2)}, u32[]{:S(2)}) collective-permute-start(f32[72,128]{1,0:T(8,128)S(1)} %get-tuple-element.25), channel_id=1, source_target_pairs={{0,1},{1,0},{2,3},{3,2},{4,5},{5,4},{6,7},{7,6},{8,9},{9,8},{10,11... | collective-permute-start | bytes 110600 | tf_op jit(solution)/shard_map/ppermute | solution.py:321
  6.0 4.6 %collective-permute-start.1 = (f32[72,128]{1,0:T(8,128)S(1)}, f32[72,128]{1,0:T(8,128)S(1)}, u32[]{:S(2)}, u32[]{:S(2)}) collective-permute-start(f32[72,128]{1,0:T(8,128)S(1)} %get-tuple-element.26), channel_id=1, source_target_pairs={{0,2},{1,3},{2,0},{3,1},{4,6},{5,7},{6,4},{7,5},{8,10},{9,11},{10,... | collective-permute-start | bytes 110600 | tf_op jit(solution)/shard_map/ppermute | solution.py:321
  8.6 3.4 %collective-permute-start.2 = (f32[72,128]{1,0:T(8,128)S(1)}, f32[72,128]{1,0:T(8,128)S(1)}, u32[]{:S(2)}, u32[]{:S(2)}) collective-permute-start(f32[72,128]{1,0:T(8,128)S(1)} %get-tuple-element.27), channel_id=1, source_target_pairs={{0,3},{1,2},{2,1},{3,0},{4,7},{5,6},{6,5},{7,4},{8,11},{9,10},{10,... | collective-permute-start | bytes 110600 | tf_op jit(solution)/shard_map/ppermute | solution.py:321
  12.0 5.8 %collective-permute-start.5 = (f32[72,128]{1,0:T(8,128)S(1)}, f32[72,128]{1,0:T(8,128)S(1)}, u32[]{:S(2)}, u32[]{:S(2)}) collective-permute-start(f32[72,128]{1,0:T(8,128)S(1)} %shard_map.97.refs_0_), channel_id=1, source_target_pairs={{0,12},{1,13},{2,14},{3,15},{4,8},{5,9},{6,10},{7,11},{8,4},{9,5},... | collective-permute-start | bytes 110600 | tf_op jit(solution)/shard_map/ppermute | solution.py:321
  15.7 4.9 %collective-permute-start.4 = (f32[72,128]{1,0:T(8,128)S(1)}, f32[72,128]{1,0:T(8,128)S(1)}, u32[]{:S(2)}, u32[]{:S(2)}) collective-permute-start(f32[72,128]{1,0:T(8,128)S(1)} %shard_map.97.refs_0_), channel_id=1, source_target_pairs={{0,8},{1,9},{2,10},{3,11},{4,12},{5,13},{6,14},{7,15},{8,0},{9,1},... | collective-permute-start | bytes 110600 | tf_op jit(solution)/shard_map/ppermute | solution.py:321
  15.7 4.9 %collective-permute-start.3 = (f32[72,128]{1,0:T(8,128)S(1)}, f32[72,128]{1,0:T(8,128)S(1)}, u32[]{:S(2)}, u32[]{:S(2)}) collective-permute-start(f32[72,128]{1,0:T(8,128)S(1)} %shard_map.97.refs_0_), channel_id=1, source_target_pairs={{0,4},{1,5},{2,6},{3,7},{4,0},{5,1},{6,2},{7,3},{8,12},{9,13},{10,... | collective-permute-start | bytes 110600 | tf_op jit(solution)/shard_map/ppermute | solution.py:321
  20.6 4.2 %collective-permute-start.8 = (f32[72,128]{1,0:T(8,128)S(1)}, f32[72,128]{1,0:T(8,128)S(1)}, u32[]{:S(2)}, u32[]{:S(2)}) collective-permute-start(f32[72,128]{1,0:T(8,128)S(1)} %shard_map.98.refs_0_), channel_id=1, source_target_pairs={{0,3},{1,2},{2,1},{3,0},{4,7},{5,6},{6,5},{7,4},{8,11},{9,10},{10,... | collective-permute-start | bytes 110600 | tf_op jit(solution)/shard_map/ppermute | solution.py:321
  20.6 4.4 %collective-permute-start.7 = (f32[72,128]{1,0:T(8,128)S(1)}, f32[72,128]{1,0:T(8,128)S(1)}, u32[]{:S(2)}, u32[]{:S(2)}) collective-permute-start(f32[72,128]{1,0:T(8,128)S(1)} %shard_map.98.refs_0_), channel_id=1, source_target_pairs={{0,2},{1,3},{2,0},{3,1},{4,6},{5,7},{6,4},{7,5},{8,10},{9,11},{10,... | collective-permute-start | bytes 110600 | tf_op jit(solution)/shard_map/ppermute | solution.py:321
  21.6 3.4 %collective-permute-start.6 = (f32[72,128]{1,0:T(8,128)S(1)}, f32[72,128]{1,0:T(8,128)S(1)}, u32[]{:S(2)}, u32[]{:S(2)}) collective-permute-start(f32[72,128]{1,0:T(8,128)S(1)} %shard_map.98.refs_0_), channel_id=1, source_target_pairs={{0,1},{1,0},{2,3},{3,2},{4,5},{5,4},{6,7},{7,6},{8,9},{9,8},{10,11... | collective-permute-start | bytes 110600 | tf_op jit(solution)/shard_map/ppermute | solution.py:321
  25.0 30.8 %copy-start.7 = (s32[16]{0:T(128)S(1)}, s32[16]{0:T(128)}, u32[]{:S(2)}) copy-start(s32[16]{0:T(128)} %angles.1) | copy-start | bytes 196
  57.6 43.8 %all-to-all-start.1 = ((f32[128,2,8,128]{3,2,1,0:T(8,128)}), f32[128,2,8,128]{3,2,1,0:T(8,128)S(1)}, u32[]{:S(2)}, u32[]{:S(2)}) async-start(f32[128,2,8,128]{3,2,1,0:T(8,128)} %bitcast.7), calls=%async_computation.1 | async-start | bytes 2097152 | tf_op jit(solution)/shard_map/all_to_all | solution.py:376
  62.6 3.9 %collective-permute-start.9 = (f32[40,128]{1,0:T(8,128)S(1)}, f32[40,128]{1,0:T(8,128)S(1)}, u32[]{:S(2)}, u32[]{:S(2)}) collective-permute-start(f32[40,128]{1,0:T(8,128)S(1)} %get-tuple-element.33), channel_id=1, source_target_pairs={{0,1},{1,0},{2,3},{3,2},{4,5},{5,4},{6,7},{7,6},{8,9},{9,8},{10,11... | collective-permute-start | bytes 61448 | tf_op jit(solution)/shard_map/ppermute | solution.py:321
  63.0 8.7 %collective-permute-start.10 = (f32[40,128]{1,0:T(8,128)S(1)}, f32[40,128]{1,0:T(8,128)S(1)}, u32[]{:S(2)}, u32[]{:S(2)}) collective-permute-start(f32[40,128]{1,0:T(8,128)S(1)} %get-tuple-element.34), channel_id=1, source_target_pairs={{0,2},{1,3},{2,0},{3,1},{4,6},{5,7},{6,4},{7,5},{8,10},{9,11},{10,... | collective-permute-start | bytes 61448 | tf_op jit(solution)/shard_map/ppermute | solution.py:321
  64.7 7.1 %collective-permute-start.11 = (f32[40,128]{1,0:T(8,128)S(1)}, f32[40,128]{1,0:T(8,128)S(1)}, u32[]{:S(2)}, u32[]{:S(2)}) collective-permute-start(f32[40,128]{1,0:T(8,128)S(1)} %get-tuple-element.35), channel_id=1, source_target_pairs={{0,3},{1,2},{2,1},{3,0},{4,7},{5,6},{6,5},{7,4},{8,11},{9,10},{10,... | collective-permute-start | bytes 61448 | tf_op jit(solution)/shard_map/ppermute | solution.py:321
  64.7 16.7 %collective-permute-start.12 = (f32[40,128]{1,0:T(8,128)S(1)}, f32[40,128]{1,0:T(8,128)S(1)}, u32[]{:S(2)}, u32[]{:S(2)}) collective-permute-start(f32[40,128]{1,0:T(8,128)S(1)} %get-tuple-element.36), channel_id=1, source_target_pairs={{0,4},{1,5},{2,6},{3,7},{4,0},{5,1},{6,2},{7,3},{8,12},{9,13},{10,... | collective-permute-start | bytes 61448 | tf_op jit(solution)/shard_map/ppermute | solution.py:321
  66.4 15.4 %collective-permute-start.13 = (f32[40,128]{1,0:T(8,128)S(1)}, f32[40,128]{1,0:T(8,128)S(1)}, u32[]{:S(2)}, u32[]{:S(2)}) collective-permute-start(f32[40,128]{1,0:T(8,128)S(1)} %get-tuple-element.37), channel_id=1, source_target_pairs={{0,5},{1,4},{2,7},{3,6},{4,1},{5,0},{6,3},{7,2},{8,13},{9,12},{10,... | collective-permute-start | bytes 61448 | tf_op jit(solution)/shard_map/ppermute | solution.py:321
  66.5 15.7 %collective-permute-start.14 = (f32[40,128]{1,0:T(8,128)S(1)}, f32[40,128]{1,0:T(8,128)S(1)}, u32[]{:S(2)}, u32[]{:S(2)}) collective-permute-start(f32[40,128]{1,0:T(8,128)S(1)} %get-tuple-element.38), channel_id=1, source_target_pairs={{0,6},{1,7},{2,4},{3,5},{4,2},{5,3},{6,0},{7,1},{8,14},{9,15},{10,... | collective-permute-start | bytes 61448 | tf_op jit(solution)/shard_map/ppermute | solution.py:321
  71.7 10.7 %collective-permute-start.15 = (f32[40,128]{1,0:T(8,128)S(1)}, f32[40,128]{1,0:T(8,128)S(1)}, u32[]{:S(2)}, u32[]{:S(2)}) collective-permute-start(f32[40,128]{1,0:T(8,128)S(1)} %get-tuple-element.39), channel_id=1, source_target_pairs={{0,7},{1,6},{2,5},{3,4},{4,3},{5,2},{6,1},{7,0},{8,15},{9,14},{10,... | collective-permute-start | bytes 61448 | tf_op jit(solution)/shard_map/ppermute | solution.py:321
  82.5 7.5 %collective-permute-start.16 = (f32[40,128]{1,0:T(8,128)S(1)}, f32[40,128]{1,0:T(8,128)S(1)}, u32[]{:S(2)}, u32[]{:S(2)}) collective-permute-start(f32[40,128]{1,0:T(8,128)S(1)} %shard_map.103.refs_0_), channel_id=1, source_target_pairs={{0,8},{1,9},{2,10},{3,11},{4,12},{5,13},{6,14},{7,15},{8,0},{9,1},... | collective-permute-start | bytes 61448 | tf_op jit(solution)/shard_map/ppermute | solution.py:321
  90.0 4.7 %collective-permute-start.23 = (f32[40,128]{1,0:T(8,128)S(1)}, f32[40,128]{1,0:T(8,128)S(1)}, u32[]{:S(2)}, u32[]{:S(2)}) collective-permute-start(f32[40,128]{1,0:T(8,128)S(1)} %shard_map.104.refs_0_), channel_id=1, source_target_pairs={{0,7},{1,6},{2,5},{3,4},{4,3},{5,2},{6,1},{7,0},{8,15},{9,14},{10,... | collective-permute-start | bytes 61448 | tf_op jit(solution)/shard_map/ppermute | solution.py:321
  90.0 5.9 %collective-permute-start.22 = (f32[40,128]{1,0:T(8,128)S(1)}, f32[40,128]{1,0:T(8,128)S(1)}, u32[]{:S(2)}, u32[]{:S(2)}) collective-permute-start(f32[40,128]{1,0:T(8,128)S(1)} %shard_map.104.refs_0_), channel_id=1, source_target_pairs={{0,6},{1,7},{2,4},{3,5},{4,2},{5,3},{6,0},{7,1},{8,14},{9,15},{10,... | collective-permute-start | bytes 61448 | tf_op jit(solution)/shard_map/ppermute | solution.py:321
  91.6 9.0 %collective-permute-start.21 = (f32[40,128]{1,0:T(8,128)S(1)}, f32[40,128]{1,0:T(8,128)S(1)}, u32[]{:S(2)}, u32[]{:S(2)}) collective-permute-start(f32[40,128]{1,0:T(8,128)S(1)} %shard_map.104.refs_0_), channel_id=1, source_target_pairs={{0,5},{1,4},{2,7},{3,6},{4,1},{5,0},{6,3},{7,2},{8,13},{9,12},{10,... | collective-permute-start | bytes 61448 | tf_op jit(solution)/shard_map/ppermute | solution.py:321
  92.9 7.6 %collective-permute-start.20 = (f32[40,128]{1,0:T(8,128)S(1)}, f32[40,128]{1,0:T(8,128)S(1)}, u32[]{:S(2)}, u32[]{:S(2)}) collective-permute-start(f32[40,128]{1,0:T(8,128)S(1)} %shard_map.104.refs_0_), channel_id=1, source_target_pairs={{0,4},{1,5},{2,6},{3,7},{4,0},{5,1},{6,2},{7,3},{8,12},{9,13},{10,... | collective-permute-start | bytes 61448 | tf_op jit(solution)/shard_map/ppermute | solution.py:321
  94.4 6.1 %collective-permute-start.19 = (f32[40,128]{1,0:T(8,128)S(1)}, f32[40,128]{1,0:T(8,128)S(1)}, u32[]{:S(2)}, u32[]{:S(2)}) collective-permute-start(f32[40,128]{1,0:T(8,128)S(1)} %shard_map.104.refs_0_), channel_id=1, source_target_pairs={{0,3},{1,2},{2,1},{3,0},{4,7},{5,6},{6,5},{7,4},{8,11},{9,10},{10,... | collective-permute-start | bytes 61448 | tf_op jit(solution)/shard_map/ppermute | solution.py:321
  94.7 5.8 %collective-permute-start.18 = (f32[40,128]{1,0:T(8,128)S(1)}, f32[40,128]{1,0:T(8,128)S(1)}, u32[]{:S(2)}, u32[]{:S(2)}) collective-permute-start(f32[40,128]{1,0:T(8,128)S(1)} %shard_map.104.refs_0_), channel_id=1, source_target_pairs={{0,2},{1,3},{2,0},{3,1},{4,6},{5,7},{6,4},{7,5},{8,10},{9,11},{10,... | collective-permute-start | bytes 61448 | tf_op jit(solution)/shard_map/ppermute | solution.py:321
  95.9 4.7 %collective-permute-start.17 = (f32[40,128]{1,0:T(8,128)S(1)}, f32[40,128]{1,0:T(8,128)S(1)}, u32[]{:S(2)}, u32[]{:S(2)}) collective-permute-start(f32[40,128]{1,0:T(8,128)S(1)} %shard_map.104.refs_0_), channel_id=1, source_target_pairs={{0,1},{1,0},{2,3},{3,2},{4,5},{5,4},{6,7},{7,6},{8,9},{9,8},{10,11... | collective-permute-start | bytes 61448 | tf_op jit(solution)/shard_map/ppermute | solution.py:321
  96.3 2.2 %copy-start = (f32[1,1024,1024]{2,1,0:T(8,128)S(1)}, f32[1,1024,1024]{2,1,0:T(8,128)}, u32[]{:S(2)}) copy-start(f32[1,1024,1024]{2,1,0:T(8,128)} %param.13) | copy-start | bytes 12582916
  99.2 1.4 %copy-start.1 = (bf16[1024,1024]{1,0:T(8,128)(2,1)}, bf16[1024,1024]{1,0:T(8,128)(2,1)S(1)}, u32[]{:S(2)}) copy-start(bf16[1024,1024]{1,0:T(8,128)(2,1)S(1)} %get-tuple-element.30.r_low_far) | copy-start | bytes 6291460
